TPU v7x, 128 devices: a whole 4x4x4 slice. The times are simulated.
128 devices in a mesh: shard: 16 (over z, x), context: 4 (over y), tensor: 2 (over core).
Axes of the slice: x: 4, y: 4, z: 4, core: 2. Of those that a mesh axis runs over, the one named last changes fastest.
Arguments:
- inputs: float32 [32, 512, 768], P('shard', 'context'), may hold values from -6 to 6
- segment_ids: int32 [32, 512], P('shard', 'context'), may hold values from 0 to 3, never falling along the last dimension, each value on 1 to 256 neighbouring positions
- projection: bfloat16 [2, 3, 768, 768], P(None, None, 'shard', 'tensor'), may hold values from -1 to 1
- head_bias: bfloat16 [2, 2, 12, 64], P(None, None, 'tensor', 'shard'), may hold values from -3 to 3
- mixing: bfloat16 [2, 768, 768], P(None, 'tensor', 'shard'), may hold values from -0.875 to 0.875
- expansion: bfloat16 [2, 768, 3072], P(None, 'shard', 'tensor'), may hold values from -0.21875 to 0.21875
- hidden_bias: bfloat16 [2, 48, 64], P(None, 'tensor', 'shard'), may hold values from -3 to 3
- contraction: bfloat16 [2, 3072, 768], P(None, 'tensor', 'shard'), may hold values from -0.109375 to 0.109375
- norm_gains: bfloat16 [2, 2, 768], P(None, None, 'shard'), may hold values from 0.3984375 to 1.59375
- offsets: bfloat16 [2, 4, 768], P(None, None, 'shard'), may hold values from -2 to 2
- cotangent: float32 [32, 512, 768], P('shard', 'context'), may hold values from -6 to 6
Outputs:
- outputs: float32 [32, 512, 768], P('shard', 'context')
- input_grad: float32 [32, 512, 768], P('shard', 'context')
- grad_projection: float32 [2, 3, 768, 768], P(None, None, 'shard', 'tensor')
- head_grad: float32 [2, 2, 12, 64], P(None, None, 'tensor', 'shard')
- grad_mixing: float32 [2, 768, 768], P(None, 'tensor', 'shard')
- grad_expansion: float32 [2, 768, 3072], P(None, 'shard', 'tensor')
- hidden_grad: float32 [2, 48, 64], P(None, 'tensor', 'shard')
- grad_contraction: float32 [2, 3072, 768], P(None, 'tensor', 'shard')
- gains_grad: float32 [2, 2, 768], P(None, None, 'shard')
- grad_offsets: float32 [2, 4, 768], P(None, None, 'shard')
Inputs may be any that keep to these rules, and one draw needn't show every extreme that they name: `segment_ids`: within a row ids never fall; every document holds 1 to 256 positions and in every row some document holds exactly 256.
All inputs are finite; a program needn't handle non-finite values.
Results may differ from a plain program's by a relative error of at most 0.033.
Values may be sent and summed in bfloat16 or wider, within the bound.
No kernel may reach another device: no remote copies, remote signals or barrier semaphores. Data moves between devices by JAX's collectives and lax.ppermute only.
A program may use at most 128 MiB of HBM per device.

v0:
```python
import jax
import jax.numpy as jnp
from jax import lax
from jax.sharding import PartitionSpec as P

HEAD = 64
EPS = 1e-05
GELU_COEF = 0.7978845608028654
GELU_CUBE = 0.044715
MASKED = -1e30
HALF = jnp.bfloat16
FULL = jnp.float32


def gelu_value(preact):
    inner_arg = GELU_COEF * (preact + GELU_CUBE * preact * preact * preact)
    return 0.5 * preact * (1.0 + jnp.tanh(inner_arg))


def gelu_slope(preact):
    inner_arg = GELU_COEF * (preact + GELU_CUBE * preact * preact * preact)
    tanh_value = jnp.tanh(inner_arg)
    return 0.5 * (1.0 + tanh_value) + 0.5 * preact * (1.0 - tanh_value * tanh_value) * GELU_COEF * (
        1.0 + 3.0 * GELU_CUBE * preact * preact
    )


def norm_forward(stream):
    center = stream - jnp.mean(stream, axis=-1, keepdims=True)
    spread = lax.rsqrt(jnp.mean(center * center, axis=-1, keepdims=True) + EPS)
    return (center * spread, spread)


def norm_backward(upstream, normed, spread, gain_row):
    scaled = upstream * gain_row
    first_mean = jnp.mean(scaled, axis=-1, keepdims=True)
    second_mean = jnp.mean(scaled * normed, axis=-1, keepdims=True)
    return spread * (scaled - first_mean - normed * second_mean)


def dot(left, right, left_dim, right_dim):
    return lax.dot_general(
        left, right, (((left_dim,), (right_dim,)), ((), ())), preferred_element_type=FULL
    )


def pair_sum(part):
    size = lax.axis_size("tensor")
    other = lax.ppermute(part, "tensor", [(i, (i + 1) % size) for i in range(size)])
    return part.astype(FULL) + other.astype(FULL)


def from_before(block, steps):
    size = lax.axis_size("context")
    return lax.ppermute(block, "context", [(i, i + steps) for i in range(size - steps)])


def from_after(block, steps):
    size = lax.axis_size("context")
    return lax.ppermute(block, "context", [(i + steps, i) for i in range(size - steps)])


def context_sum(part):
    size = lax.axis_size("context")
    total = part.astype(FULL)
    for steps in range(1, size):
        moved = lax.ppermute(part, "context", [(i, (i + steps) % size) for i in range(size)])
        total = total + moved.astype(FULL)
    return total


def masked_scores(query_block, key_block, visible, head_scale):
    scores = (
        jnp.einsum("rqhe,rkhe->rhqk", query_block, key_block, preferred_element_type=FULL)
        * head_scale
    )
    return jnp.where(visible, scores, MASKED)


def per_device(
    inputs,
    segment_ids,
    projection,
    head_bias,
    mixing,
    expansion,
    hidden_bias,
    contraction,
    norm_gains,
    offsets,
    cotangent,
):
    layers = projection.shape[0]
    rows, block, width = inputs.shape
    shards = lax.axis_size("shard")
    contexts = lax.axis_size("context")
    own = projection.shape[2]
    heads = head_bias.shape[2]
    head_cols = projection.shape[3]
    hidden = expansion.shape[2]
    tokens = rows * block
    head_scale = HEAD ** (-0.5)
    back_steps = 2
    gathered = []
    for layer in range(layers):
        packed = jnp.concatenate(
            [
                projection[layer, 0],
                projection[layer, 1],
                projection[layer, 2],
                mixing[layer].T,
                expansion[layer],
                contraction[layer].T,
            ],
            axis=1,
        )
        gathered.append(lax.all_gather(packed, "shard", axis=0, tiled=True))
    small_parts = [norm_gains, offsets, head_bias, hidden_bias]
    small_sizes = [part.size for part in small_parts]
    small_total = sum(small_sizes)
    small_padded = -(-small_total // 1024) * 1024
    small = jnp.concatenate(
        [part.reshape(-1) for part in small_parts]
        + [jnp.zeros((small_padded - small_total,), HALF)]
    )
    small = jnp.broadcast_to(small.reshape(1, -1, 128), (shards, small_padded // 128, 128))
    small = lax.all_to_all(small, "shard", 0, 0).reshape(shards, small_padded)

    def widen(index):
        start = sum(small_sizes[:index])
        shape = small_parts[index].shape
        piece = small[:, start : start + small_sizes[index]].astype(FULL).reshape((shards,) + shape)
        piece = jnp.moveaxis(piece, 0, -2)
        return piece.reshape(shape[:-1] + (shards * shape[-1],))

    gains_all, offsets_all = (widen(0), widen(1))
    head_all = widen(2).reshape(layers, 2, head_cols)
    hidden_all = widen(3).reshape(layers, hidden)
    seg_before = [from_before(segment_ids, steps) for steps in range(back_steps, 0, -1)]
    segments_all = jnp.concatenate(seg_before + [segment_ids], axis=1)
    query_pos = jnp.arange(block, dtype=jnp.int32) + back_steps * block
    key_pos = jnp.arange((back_steps + 1) * block, dtype=jnp.int32)
    first_key = (back_steps - lax.axis_index("context")) * block
    visible = (
        (segments_all[:, None, :] == segment_ids[:, :, None])
        & (key_pos[None, None, :] <= query_pos[None, :, None])
        & (key_pos >= first_key)[None, None, :]
    )
    visible = visible[:, None]

    def split_weights(weights):
        ends = [3 * head_cols, 4 * head_cols, 4 * head_cols + hidden, 4 * head_cols + 2 * hidden]
        return (
            weights[:, : ends[0]],
            weights[:, ends[0] : ends[1]],
            weights[:, ends[1] : ends[2]],
            weights[:, ends[2] : ends[3]],
        )

    stream = inputs.reshape(tokens, width)
    kept = []
    for layer in range(layers):
        qkv_weight, out_weight, up_weight, down_weight = split_weights(gathered[layer])
        gain, offset = (gains_all[layer], offsets_all[layer])
        normed_one, spread_one = norm_forward(stream)
        attend_input = (normed_one * gain[0] + offset[0]).astype(HALF)
        zero_bias = jnp.zeros((head_cols,), FULL)
        bias = jnp.concatenate([head_all[layer, 0], zero_bias, head_all[layer, 1]])
        projected = (dot(attend_input, qkv_weight, 1, 0) + bias).astype(HALF)
        query_rows = projected[:, :head_cols]
        key_value = projected[:, head_cols:].reshape(rows, block, 2 * head_cols)
        before = [from_before(key_value, steps) for steps in range(back_steps, 0, -1)]
        key_value_all = jnp.concatenate(before + [key_value], axis=1)
        query_block = query_rows.reshape(rows, block, heads, HEAD)
        key_block = key_value_all[:, :, :head_cols].reshape(rows, -1, heads, HEAD)
        value_block = key_value_all[:, :, head_cols:].reshape(rows, -1, heads, HEAD)
        masked = masked_scores(query_block, key_block, visible, head_scale)
        row_top = jnp.max(masked, axis=-1, keepdims=True)
        log_total = row_top + jnp.log(jnp.sum(jnp.exp(masked - row_top), axis=-1, keepdims=True))
        soft_half = jnp.exp(masked - log_total).astype(HALF)
        attended = (
            jnp.einsum("rhqk,rkhe->rqhe", soft_half, value_block, preferred_element_type=FULL)
            .astype(HALF)
            .reshape(tokens, head_cols)
        )
        middle = stream + pair_sum(dot(attended, out_weight, 1, 1)) + offset[2]
        normed_two, spread_two = norm_forward(middle)
        feed_input = (normed_two * gain[1] + offset[1]).astype(HALF)
        preact = dot(feed_input, up_weight, 1, 0) + hidden_all[layer]
        activation = gelu_value(preact).astype(HALF)
        stream = middle + pair_sum(dot(activation, down_weight, 1, 1)) + offset[3]
        kept.append(
            (
                normed_one,
                spread_one,
                attend_input,
                query_block,
                key_block,
                value_block,
                log_total,
                attended,
                normed_two,
                spread_two,
                feed_input,
                preact,
                activation,
            )
        )

    def scatter(parts):
        packed = jnp.concatenate([part.astype(HALF) for part in parts], axis=1)
        return lax.psum_scatter(packed, "shard", scatter_dimension=0, tiled=True)

    upstream = cotangent.reshape(tokens, width)
    feed_shares, attend_shares, vectors = ([None] * layers, [None] * layers, [None] * layers)
    for layer in reversed(range(layers)):
        (
            normed_one,
            spread_one,
            attend_input,
            query_block,
            key_block,
            value_block,
            log_total,
            attended,
            normed_two,
            spread_two,
            feed_input,
            preact,
            activation,
        ) = kept[layer]
        qkv_weight, out_weight, up_weight, down_weight = split_weights(gathered[layer])
        gain = gains_all[layer]
        upstream_half = upstream.astype(HALF)
        contraction_part = dot(upstream_half, activation, 0, 0)
        offset_down = jnp.sum(upstream, axis=0)
        hidden_back = dot(upstream_half, down_weight, 1, 0) * gelu_slope(preact)
        hidden_half = hidden_back.astype(HALF)
        hidden_part = jnp.sum(hidden_back, axis=0)
        expansion_part = dot(feed_input, hidden_half, 0, 0)
        feed_shares[layer] = scatter([expansion_part, contraction_part])
        feed_back = pair_sum(dot(hidden_half, up_weight, 1, 1).astype(HALF))
        gain_two = jnp.sum(feed_back * normed_two, axis=0)
        offset_two = jnp.sum(feed_back, axis=0)
        middle_back = upstream + norm_backward(feed_back, normed_two, spread_two, gain[1])
        middle_half = middle_back.astype(HALF)
        mixing_part = dot(middle_half, attended, 0, 0)
        offset_mix = jnp.sum(middle_back, axis=0)
        attended_back = dot(middle_half, out_weight, 1, 0).astype(HALF)
        back_heads = attended_back.reshape(rows, block, heads, HEAD)
        attended_heads = attended.reshape(rows, block, heads, HEAD)
        row_delta = jnp.sum(back_heads.astype(FULL) * attended_heads.astype(FULL), axis=-1)
        masked = masked_scores(query_block, key_block, visible, head_scale)
        soft = jnp.exp(masked - log_total)
        soft_half = soft.astype(HALF)
        prob_back = jnp.einsum(
            "rqhe,rkhe->rhqk", back_heads, value_block, preferred_element_type=FULL
        )
        score_back = (
            soft * (prob_back - jnp.transpose(row_delta, (0, 2, 1))[..., None]) * head_scale
        ).astype(HALF)
        query_back = jnp.einsum(
            "rhqk,rkhe->rqhe", score_back, key_block, preferred_element_type=FULL
        ).reshape(tokens, head_cols)
        key_full = jnp.einsum(
            "rhqk,rqhe->rkhe", score_back, query_block, preferred_element_type=FULL
        ).reshape(rows, -1, head_cols)
        value_full = jnp.einsum(
            "rhqk,rqhe->rkhe", soft_half, back_heads, preferred_element_type=FULL
        ).reshape(rows, -1, head_cols)
        both_full = jnp.concatenate([key_full, value_full], axis=2)
        both_back = both_full[:, back_steps * block :]
        for steps in range(1, back_steps + 1):
            start = (back_steps - steps) * block
            both_back = both_back + from_after(
                both_full[:, start : start + block].astype(HALF), steps
            ).astype(FULL)
        both_back = both_back.reshape(tokens, 2 * head_cols)
        head_part = jnp.concatenate(
            [jnp.sum(query_back, axis=0), jnp.sum(both_back[:, head_cols:], axis=0)]
        )
        project_back = jnp.concatenate([query_back, both_back], axis=1).astype(HALF)
        projection_part = dot(attend_input, project_back, 0, 0)
        attend_shares[layer] = scatter([projection_part, mixing_part])
        input_back = pair_sum(dot(project_back, qkv_weight, 1, 1).astype(HALF))
        gain_one = jnp.sum(input_back * normed_one, axis=0)
        offset_one = jnp.sum(input_back, axis=0)
        upstream = middle_back + norm_backward(input_back, normed_one, spread_one, gain[0])
        vectors[layer] = (
            [gain_one, gain_two],
            [offset_one, offset_two, offset_mix, offset_down],
            head_part,
            hidden_part,
        )

    def spread_out(values, shape):
        lead = shape[:-1]
        values = values.reshape(lead + (shards, shape[-1]))
        return jnp.moveaxis(values, -2, 0).reshape(shards, -1)

    gain_sums = jnp.stack([jnp.stack(entry[0]) for entry in vectors])
    offset_sums = jnp.stack([jnp.stack(entry[1]) for entry in vectors])
    head_sums = jnp.stack([entry[2] for entry in vectors])
    hidden_sums = jnp.stack([entry[3] for entry in vectors])
    vector_pack = jnp.concatenate(
        [
            spread_out(values, part.shape)
            for values, part in zip((gain_sums, offset_sums, head_sums, hidden_sums), small_parts)
        ]
        + [jnp.zeros((shards, small_padded - small_total), FULL)],
        axis=1,
    )
    vector_pack = lax.all_to_all(vector_pack.reshape(shards, -1, 128), "shard", 0, 0)
    vector_own = context_sum(jnp.sum(vector_pack, axis=0)).reshape(-1)
    vector_out = []
    for index, part in enumerate(small_parts):
        start = sum(small_sizes[:index])
        vector_out.append(vector_own[start : start + small_sizes[index]].reshape(part.shape))
    gains_grad, offsets_grad, head_grad, hidden_grad = vector_out
    feed_own = [context_sum(share) for share in feed_shares]
    attend_own = [context_sum(share) for share in attend_shares]
    projection_grad = jnp.stack(
        [
            jnp.stack([share[:, k * head_cols : (k + 1) * head_cols] for k in range(3)])
            for share in attend_own
        ]
    )
    mixing_grad = jnp.stack([share[:, 3 * head_cols :].T for share in attend_own])
    expansion_grad = jnp.stack([share[:, :hidden] for share in feed_own])
    contraction_grad = jnp.stack([share[:, hidden:].T for share in feed_own])
    return (
        stream.reshape(rows, block, width),
        upstream.reshape(rows, block, width),
        projection_grad,
        head_grad,
        mixing_grad,
        expansion_grad,
        hidden_grad,
        contraction_grad,
        gains_grad,
        offsets_grad,
    )


def solution(mesh):
    in_specs = (
        P("shard", "context", None),
        P("shard", "context"),
        P(None, None, "shard", "tensor"),
        P(None, None, "tensor", "shard"),
        P(None, "tensor", "shard"),
        P(None, "shard", "tensor"),
        P(None, "tensor", "shard"),
        P(None, "tensor", "shard"),
        P(None, None, "shard"),
        P(None, None, "shard"),
        P("shard", "context", None),
    )
    out_specs = (
        P("shard", "context", None),
        P("shard", "context", None),
        P(None, None, "shard", "tensor"),
        P(None, None, "tensor", "shard"),
        P(None, "tensor", "shard"),
        P(None, "shard", "tensor"),
        P(None, "tensor", "shard"),
        P(None, "tensor", "shard"),
        P(None, None, "shard"),
        P(None, None, "shard"),
    )
    return jax.shard_map(
        per_device, mesh=mesh, in_specs=in_specs, out_specs=out_specs, check_vma=False
    )
```

profile of v0, /device:TPU:0, one launch (start us, length us, event | category | flops | bytes accessed | tf_op | source)
XLA Modules:
  0.0 616.7 jit_solution(8124101954752828164)
XLA Ops:
  14.1 5.2 collective-permute-start.2
  19.3 2.6 collective-permute-start.3
  23.3 7.9 %all-to-all-start = ((bf16[16,8,128]{2,1,0:T(8,128)(2,1)}), bf16[16,8,128]{2,1,0:T(8,128)(2,1)S(1)}, u32[]{:S(2)}, u32[]{:S(2)}) async-start(bf16[16,8,128]{2,1,0:T(8,128)(2,1)} %broadcast_in_dim.34), calls=%async_computation | async-start | bytes 65536 | tf_op jit(solution)/shard_map/all_to_all | solution.py:127
  31.7 7.1 %all-to-all-done = bf16[16,8,128]{2,1,0:T(8,128)(2,1)S(1)} async-done(((bf16[16,8,128]{2,1,0:T(8,128)(2,1)}), bf16[16,8,128]{2,1,0:T(8,128)(2,1)S(1)}, u32[]{:S(2)}, u32[]{:S(2)}) %all-to-all-start) | async-done | bytes 32800 | tf_op jit(solution)/shard_map/all_to_all | solution.py:127
  42.3 39.0 %all-gather.3.cloned.1.call-done = bf16[768,4608]{1,0:T(8,128)(2,1)} async-done(((bf16[48,4608]{1,0:T(8,128)(2,1)}), bf16[768,4608]{1,0:T(8,128)(2,1)}) %all-gather.3.cloned.1.call-update) | async-done | bytes 7077904 | tf_op jit(solution)/shard_map/all_gather | solution.py:117
  83.5 4.9 collective-permute-start
  88.4 2.5 collective-permute-start.1
  91.4 6.5 %collective-permute-done = bf16[2,128,768]{2,1,0:T(8,128)(2,1)S(1)} collective-permute-done((bf16[2,128,768]{2,1,0:T(8,128)(2,1)S(1)}, bf16[2,128,768]{2,1,0:T(8,128)(2,1)S(1)}, u32[]{:S(2)}, u32[]{:S(2)}) %collective-permute-start) | collective-permute-done | bytes 393248 | tf_op jit(solution)/shard_map/ppermute | solution.py:55
  97.9 7.3 %collective-permute-done.1 = bf16[2,128,768]{2,1,0:T(8,128)(2,1)S(1)} collective-permute-done((bf16[2,128,768]{2,1,0:T(8,128)(2,1)S(1)}, bf16[2,128,768]{2,1,0:T(8,128)(2,1)S(1)}, u32[]{:S(2)}, u32[]{:S(2)}) %collective-permute-start.1) | collective-permute-done | bytes 393248 | tf_op jit(solution)/shard_map/ppermute | solution.py:55
  126.0 2.6 convolution_add_fusion.3
  128.6 4.2 fusion.15
  138.5 10.1 %all-gather.5.cloned.1.call-done = bf16[768,4608]{1,0:T(8,128)(2,1)} async-done(((bf16[48,4608]{1,0:T(8,128)(2,1)}), bf16[768,4608]{1,0:T(8,128)(2,1)}) %all-gather.5.cloned.1.call-update) | async-done | bytes 7077904 | tf_op jit(solution)/shard_map/all_gather | solution.py:117
  151.9 5.7 collective-permute-start.6
  157.6 3.4 collective-permute-start.7
  162.8 3.9 collective-permute-done.6
  166.7 7.3 %collective-permute-done.7 = bf16[2,128,768]{2,1,0:T(8,128)(2,1)} collective-permute-done((bf16[2,128,768]{2,1,0:T(8,128)(2,1)}, bf16[2,128,768]{2,1,0:T(8,128)(2,1)}, u32[]{:S(2)}, u32[]{:S(2)}) %collective-permute-start.7) | collective-permute-done | bytes 393248 | tf_op jit(solution)/shard_map/ppermute | solution.py:55
  184.6 2.6 fusion.49
  200.9 2.7 convolution_add_fusion.2
  203.6 4.2 fusion.135
  212.3 2.5 multiply_reduce_fusion
  214.8 3.5 fusion.119
  223.5 3.5 fusion.80
  228.9 2.7 copy.186
  231.6 2.6 fusion.100
  234.2 2.7 copy.185
  246.2 7.9 %collective-permute-done.11 = bf16[2,128,768]{2,1,0:T(8,128)(2,1)} collective-permute-done((bf16[2,128,768]{2,1,0:T(8,128)(2,1)}, bf16[2,128,768]{2,1,0:T(8,128)(2,1)}, u32[]{:S(2)}, u32[]{:S(2)}) %collective-permute-start.11) | collective-permute-done | bytes 393248 | tf_op jit(solution)/shard_map/ppermute | solution.py:60
  254.1 3.1 collective-permute-done.12
  272.3 2.5 multiply_reduce_fusion.2
  282.7 2.7 copy.195
  298.5 15.0 %collective-permute-done.15 = bf16[2,128,768]{2,1,0:T(8,128)(2,1)} collective-permute-done((bf16[2,128,768]{2,1,0:T(8,128)(2,1)}, bf16[2,128,768]{2,1,0:T(8,128)(2,1)}, u32[]{:S(2)}, u32[]{:S(2)}) %collective-permute-start.15) | collective-permute-done | bytes 393248 | tf_op jit(solution)/shard_map/ppermute | solution.py:60
  313.5 3.2 collective-permute-done.16
  325.4 2.7 pad_maximum_fusion.1
  332.5 2.7 pad_maximum_fusion
  352.5 5.3 all-to-all-start.1
  357.8 7.6 %all-to-all-done.1 = f32[16,8,128]{2,1,0:T(8,128)S(1)} async-done(((f32[16,8,128]{2,1,0:T(8,128)}), f32[16,8,128]{2,1,0:T(8,128)S(1)}, u32[]{:S(2)}, u32[]{:S(2)}) %all-to-all-start.1) | async-done | bytes 65568 | tf_op jit(solution)/shard_map/all_to_all | solution.py:313
  365.5 7.0 %collective-permute-start.24 = (f32[8,128]{1,0:T(8,128)S(1)}, f32[8,128]{1,0:T(8,128)S(1)}, u32[]{:S(2)}, u32[]{:S(2)}) collective-permute-start(f32[8,128]{1,0:T(8,128)S(1)} %reduce_sum.395), channel_id=1, source_target_pairs={{0,2},{2,4},{4,6},{6,0},{1,3},{3,5},{5,7},{7,1},{8,10},{10,12},{12... | collective-permute-start | bytes 12296 | tf_op jit(solution)/shard_map/ppermute | solution.py:67
  372.5 2.8 collective-permute-start.26
  377.8 3.8 collective-permute-start.22
  388.0 41.1 %reduce-scatter.5.cloned.1.call-done = bf16[48,1536]{1,0:T(8,128)(2,1)} async-done(((bf16[768,1536]{1,0:T(8,128)(2,1)}), bf16[48,1536]{1,0:T(8,128)(2,1)}) %reduce-scatter.5.cloned.1.call-update) | async-done | bytes 147472 | tf_op jit(solution)/shard_map/reduce_scatter | solution.py:212
  430.6 2.7 collective-permute-start.19
  439.6 70.3 %reduce-scatter.11.cloned.1.call-done = bf16[48,3072]{1,0:T(8,128)(2,1)} async-done(((bf16[768,3072]{1,0:T(8,128)(2,1)}), bf16[48,3072]{1,0:T(8,128)(2,1)}) %reduce-scatter.11.cloned.1.call-update) | async-done | bytes 294928 | tf_op jit(solution)/shard_map/reduce_scatter | solution.py:212
  511.4 2.7 collective-permute-start.31
  517.1 3.2 collective-permute-done.30
  520.3 5.5 collective-permute-done.31
  526.0 64.9 %reduce-scatter.9.cloned.1.call-done = bf16[48,3072]{1,0:T(8,128)(2,1)} async-done(((bf16[768,3072]{1,0:T(8,128)(2,1)}), bf16[48,3072]{1,0:T(8,128)(2,1)}) %reduce-scatter.9.cloned.1.call-update) | async-done | bytes 294928 | tf_op jit(solution)/shard_map/reduce_scatter | solution.py:212
  592.3 2.7 collective-permute-start.28
  596.5 4.8 collective-permute-done.27
  601.3 5.5 collective-permute-done.28
  (514 shorter events, 183.7 us)
Async XLA Ops:
  7.2 24.0 %copy-start.2 = (f32[2,128,768]{2,1,0:T(8,128)S(1)}, f32[2,128,768]{2,1,0:T(8,128)}, u32[]{:S(2)}) copy-start(f32[2,128,768]{2,1,0:T(8,128)} %param.11) | copy-start | bytes 2359300
  7.2 74.0 %all-gather.3.cloned.1.call-start = ((), (), s32[]{:S(2)}) async-start(), calls=%async_computation.6 | async-start | bytes 7520256 | tf_op jit(solution)/shard_map/all_gather | solution.py:117
  13.4 135.2 %all-gather.5.cloned.1.call-start = ((), (), s32[]{:S(2)}) async-start(), calls=%async_computation.7 | async-start | bytes 7520256 | tf_op jit(solution)/shard_map/all_gather | solution.py:117
  14.1 76.8 %collective-permute-start.2 = (s32[2,128]{1,0:T(2,128)S(1)}, s32[2,128]{1,0:T(2,128)S(1)}, u32[]{:S(2)}, u32[]{:S(2)}) collective-permute-start(s32[2,128]{1,0:T(2,128)S(1)} %copy-done.105), channel_id=1, source_target_pairs={{0,4},{2,6},{1,5},{3,7},{8,12},{10,14},{9,13},{11,15},{16,20},{18,... | collective-permute-start | bytes 3080 | tf_op jit(solution)/shard_map/ppermute | solution.py:55
  19.3 71.7 %collective-permute-start.3 = (s32[2,128]{1,0:T(2,128)S(1)}, s32[2,128]{1,0:T(2,128)S(1)}, u32[]{:S(2)}, u32[]{:S(2)}) collective-permute-start(s32[2,128]{1,0:T(2,128)S(1)} %copy-done.105), channel_id=1, source_target_pairs={{0,2},{2,4},{4,6},{1,3},{3,5},{5,7},{8,10},{10,12},{12,14},{9,11},... | collective-permute-start | bytes 3080 | tf_op jit(solution)/shard_map/ppermute | solution.py:55
  23.3 15.6 %all-to-all-start = ((bf16[16,8,128]{2,1,0:T(8,128)(2,1)}), bf16[16,8,128]{2,1,0:T(8,128)(2,1)S(1)}, u32[]{:S(2)}, u32[]{:S(2)}) async-start(bf16[16,8,128]{2,1,0:T(8,128)(2,1)} %broadcast_in_dim.34), calls=%async_computation | async-start | bytes 65536 | tf_op jit(solution)/shard_map/all_to_all | solution.py:127
  31.2 346.6 %reduce-scatter.7.cloned.1.call-start = ((), (), s32[]{:S(2)}) async-start(), calls=%async_computation.9 | async-start | bytes 2506752 | tf_op jit(solution)/shard_map/reduce_scatter | solution.py:212
  31.4 52.0 %copy-start.80 = (f32[256]{0:T(256)}, f32[256]{0:T(256)S(1)}, u32[]{:S(2)}) copy-start(f32[256]{0:T(256)S(1)} %get-tuple-element.151) | copy-start | bytes 3076
  31.7 51.7 %copy-start.82 = (f32[256]{0:T(256)}, f32[256]{0:T(256)S(1)}, u32[]{:S(2)}) copy-start(f32[256]{0:T(256)S(1)} %rsqrt_bitcast_fusion) | copy-start | bytes 3076
  40.8 42.6 %copy-start.58 = (f32[768]{0:T(1024)}, f32[768]{0:T(1024)S(1)}, u32[]{:S(2)}) copy-start(f32[768]{0:T(1024)S(1)} %mul.315) | copy-start | bytes 9220
  42.3 39.0 %copy-start.42 = (bf16[256,768]{1,0:T(8,128)(2,1)}, bf16[256,768]{1,0:T(8,128)(2,1)S(1)}, u32[]{:S(2)}) copy-start(bf16[256,768]{1,0:T(8,128)(2,1)S(1)} %add_convert_fusion.3) | copy-start | bytes 1179652
  83.5 14.5 %collective-permute-start = (bf16[2,128,768]{2,1,0:T(8,128)(2,1)S(1)}, bf16[2,128,768]{2,1,0:T(8,128)(2,1)S(1)}, u32[]{:S(2)}, u32[]{:S(2)}) collective-permute-start(bf16[2,128,768]{2,1,0:T(8,128)(2,1)S(1)} %bitcast.247), channel_id=1, source_target_pairs={{0,4},{2,6},{1,5},{3,7},{8,12},{10,14},{9,13},{11,15},{16,20},{18,... | collective-permute-start | bytes 1179656 | tf_op jit(solution)/shard_map/ppermute | solution.py:55
  88.4 16.8 %collective-permute-start.1 = (bf16[2,128,768]{2,1,0:T(8,128)(2,1)S(1)}, bf16[2,128,768]{2,1,0:T(8,128)(2,1)S(1)}, u32[]{:S(2)}, u32[]{:S(2)}) collective-permute-start(bf16[2,128,768]{2,1,0:T(8,128)(2,1)S(1)} %bitcast.248), channel_id=1, source_target_pairs={{0,2},{2,4},{4,6},{1,3},{3,5},{5,7},{8,10},{10,12},{12,14},{9,11},... | collective-permute-start | bytes 1179656 | tf_op jit(solution)/shard_map/ppermute | solution.py:55
  114.4 8.5 %collective-permute-start.4 = (f32[256,768]{1,0:T(8,128)}, f32[256,768]{1,0:T(8,128)}, u32[]{:S(2)}, u32[]{:S(2)}) collective-permute-start(f32[256,768]{1,0:T(8,128)} %fusion.74), channel_id=1, source_target_pairs={{0,1},{1,0},{2,3},{3,2},{4,5},{5,4},{6,7},{7,6},{8,9},{9,8},{10,11... | collective-permute-start | bytes 2359304 | tf_op jit(solution)/shard_map/ppermute | solution.py:49
  132.9 2.7 collective-permute-start.5
  151.9 14.8 %collective-permute-start.6 = (bf16[2,128,768]{2,1,0:T(8,128)(2,1)}, bf16[2,128,768]{2,1,0:T(8,128)(2,1)}, u32[]{:S(2)}, u32[]{:S(2)}) collective-permute-start(bf16[2,128,768]{2,1,0:T(8,128)(2,1)} %bitcast.30), channel_id=1, source_target_pairs={{0,4},{2,6},{1,5},{3,7},{8,12},{10,14},{9,13},{11,15},{16,20},{18,... | collective-permute-start | bytes 1179656 | tf_op jit(solution)/shard_map/ppermute | solution.py:55
  157.6 16.4 %collective-permute-start.7 = (bf16[2,128,768]{2,1,0:T(8,128)(2,1)}, bf16[2,128,768]{2,1,0:T(8,128)(2,1)}, u32[]{:S(2)}, u32[]{:S(2)}) collective-permute-start(bf16[2,128,768]{2,1,0:T(8,128)(2,1)} %bitcast.30), channel_id=1, source_target_pairs={{0,2},{2,4},{4,6},{1,3},{3,5},{5,7},{8,10},{10,12},{12,14},{9,11},... | collective-permute-start | bytes 1179656 | tf_op jit(solution)/shard_map/ppermute | solution.py:55
  189.9 8.8 %collective-permute-start.8 = (f32[256,768]{1,0:T(8,128)}, f32[256,768]{1,0:T(8,128)}, u32[]{:S(2)}, u32[]{:S(2)}) collective-permute-start(f32[256,768]{1,0:T(8,128)} %fusion.71), channel_id=1, source_target_pairs={{0,1},{1,0},{2,3},{3,2},{4,5},{5,4},{6,7},{7,6},{8,9},{9,8},{10,11... | collective-permute-start | bytes 2359304 | tf_op jit(solution)/shard_map/ppermute | solution.py:49
  209.5 2.8 collective-permute-start.10
  212.0 2.8 collective-permute-start.9
  239.6 14.4 %collective-permute-start.11 = (bf16[2,128,768]{2,1,0:T(8,128)(2,1)}, bf16[2,128,768]{2,1,0:T(8,128)(2,1)}, u32[]{:S(2)}, u32[]{:S(2)}) collective-permute-start(bf16[2,128,768]{2,1,0:T(8,128)(2,1)} %get-tuple-element.106), channel_id=1, source_target_pairs={{2,0},{4,2},{6,4},{3,1},{5,3},{7,5},{10,8},{12,10},{14,12},{11,9},... | collective-permute-start | bytes 1179656 | tf_op jit(solution)/shard_map/ppermute | solution.py:60
  240.9 16.2 %collective-permute-start.12 = (bf16[2,128,768]{2,1,0:T(8,128)(2,1)}, bf16[2,128,768]{2,1,0:T(8,128)(2,1)}, u32[]{:S(2)}, u32[]{:S(2)}) collective-permute-start(bf16[2,128,768]{2,1,0:T(8,128)(2,1)} %get-tuple-element.107), channel_id=1, source_target_pairs={{4,0},{6,2},{5,1},{7,3},{12,8},{14,10},{13,9},{15,11},{20,16},{22,... | collective-permute-start | bytes 1179656 | tf_op jit(solution)/shard_map/ppermute | solution.py:60
  262.1 2.0 collective-permute-start.13
  270.0 2.1 collective-permute-start.14
  271.7 157.4 %reduce-scatter.5.cloned.1.call-start = ((), (), s32[]{:S(2)}) async-start(), calls=%async_computation.8 | async-start | bytes 2506752 | tf_op jit(solution)/shard_map/reduce_scatter | solution.py:212
  293.6 20.0 %collective-permute-start.15 = (bf16[2,128,768]{2,1,0:T(8,128)(2,1)}, bf16[2,128,768]{2,1,0:T(8,128)(2,1)}, u32[]{:S(2)}, u32[]{:S(2)}) collective-permute-start(bf16[2,128,768]{2,1,0:T(8,128)(2,1)} %get-tuple-element.104), channel_id=1, source_target_pairs={{2,0},{4,2},{6,4},{3,1},{5,3},{7,5},{10,8},{12,10},{14,12},{11,9},... | collective-permute-start | bytes 1179656 | tf_op jit(solution)/shard_map/ppermute | solution.py:60
  294.9 21.9 %collective-permute-start.16 = (bf16[2,128,768]{2,1,0:T(8,128)(2,1)}, bf16[2,128,768]{2,1,0:T(8,128)(2,1)}, u32[]{:S(2)}, u32[]{:S(2)}) collective-permute-start(bf16[2,128,768]{2,1,0:T(8,128)(2,1)} %get-tuple-element.105), channel_id=1, source_target_pairs={{4,0},{6,2},{5,1},{7,3},{12,8},{14,10},{13,9},{15,11},{20,16},{22,... | collective-permute-start | bytes 1179656 | tf_op jit(solution)/shard_map/ppermute | solution.py:60
  298.1 20.8 %copy-start.48 = (bf16[256,384]{1,0:T(8,128)(2,1)}, bf16[256,384]{1,0:T(8,128)(2,1)S(1)}, u32[]{:S(2)}) copy-start(bf16[256,384]{1,0:T(8,128)(2,1)S(1)} %copy.196) | copy-start | bytes 589828
  321.3 188.7 %reduce-scatter.11.cloned.1.call-start = ((), (), s32[]{:S(2)}) async-start(), calls=%async_computation.11 | async-start | bytes 5013504 | tf_op jit(solution)/shard_map/reduce_scatter | solution.py:212
  328.2 262.7 %reduce-scatter.9.cloned.1.call-start = ((), (), s32[]{:S(2)}) async-start(), calls=%async_computation.10 | async-start | bytes 5013504 | tf_op jit(solution)/shard_map/reduce_scatter | solution.py:212
  343.3 6.8 %collective-permute-start.17 = (bf16[256,768]{1,0:T(8,128)(2,1)S(1)}, bf16[256,768]{1,0:T(8,128)(2,1)S(1)}, u32[]{:S(2)}, u32[]{:S(2)}) collective-permute-start(bf16[256,768]{1,0:T(8,128)(2,1)S(1)} %fusion.36), channel_id=1, source_target_pairs={{0,1},{1,0},{2,3},{3,2},{4,5},{5,4},{6,7},{7,6},{8,9},{9,8},{10,11... | collective-permute-start | bytes 1179656 | tf_op jit(solution)/shard_map/ppermute | solution.py:49
  349.0 26.3 %copy-start.83 = (f32[256]{0:T(256)S(1)}, f32[256]{0:T(256)}, u32[]{:S(2)}) copy-start(f32[256]{0:T(256)} %copy-done.82) | copy-start | bytes 3076
  352.5 12.9 %all-to-all-start.1 = ((f32[16,8,128]{2,1,0:T(8,128)}), f32[16,8,128]{2,1,0:T(8,128)S(1)}, u32[]{:S(2)}, u32[]{:S(2)}) async-start(f32[16,8,128]{2,1,0:T(8,128)} %bitcast.123), calls=%async_computation.3 | async-start | bytes 131072 | tf_op jit(solution)/shard_map/all_to_all | solution.py:313
  365.5 11.0 %collective-permute-start.24 = (f32[8,128]{1,0:T(8,128)S(1)}, f32[8,128]{1,0:T(8,128)S(1)}, u32[]{:S(2)}, u32[]{:S(2)}) collective-permute-start(f32[8,128]{1,0:T(8,128)S(1)} %reduce_sum.395), channel_id=1, source_target_pairs={{0,2},{2,4},{4,6},{6,0},{1,3},{3,5},{5,7},{7,1},{8,10},{10,12},{12... | collective-permute-start | bytes 12296 | tf_op jit(solution)/shard_map/ppermute | solution.py:67
  372.5 5.1 collective-permute-start.25
  372.5 5.1 collective-permute-start.26
  377.7 7.7 %collective-permute-start.21 = (bf16[48,1536]{1,0:T(8,128)(2,1)}, bf16[48,1536]{1,0:T(8,128)(2,1)S(1)}, u32[]{:S(2)}, u32[]{:S(2)}) collective-permute-start(bf16[48,1536]{1,0:T(8,128)(2,1)} %reduce-scatter.7.cloned.1.call-done), channel_id=1, source_target_pairs={{0,2},{2,4},{4,6},{6,0},{1,3},{3,5},{5,7},{7,1},{8,10},{10,12},{12... | collective-permute-start | bytes 442376 | tf_op jit(solution)/shard_map/ppermute | solution.py:67
  377.8 8.8 %collective-permute-start.22 = (bf16[48,1536]{1,0:T(8,128)(2,1)}, bf16[48,1536]{1,0:T(8,128)(2,1)S(1)}, u32[]{:S(2)}, u32[]{:S(2)}) collective-permute-start(bf16[48,1536]{1,0:T(8,128)(2,1)} %reduce-scatter.7.cloned.1.call-done), channel_id=1, source_target_pairs={{0,4},{2,6},{4,0},{6,2},{1,5},{3,7},{5,1},{7,3},{8,12},{10,14},{12... | collective-permute-start | bytes 442376 | tf_op jit(solution)/shard_map/ppermute | solution.py:67
  381.7 5.4 collective-permute-start.23
  429.1 7.9 %collective-permute-start.18 = (bf16[48,1536]{1,0:T(8,128)(2,1)}, bf16[48,1536]{1,0:T(8,128)(2,1)S(1)}, u32[]{:S(2)}, u32[]{:S(2)}) collective-permute-start(bf16[48,1536]{1,0:T(8,128)(2,1)} %reduce-scatter.5.cloned.1.call-done), channel_id=1, source_target_pairs={{0,2},{2,4},{4,6},{6,0},{1,3},{3,5},{5,7},{7,1},{8,10},{10,12},{12... | collective-permute-start | bytes 442376 | tf_op jit(solution)/shard_map/ppermute | solution.py:67
  430.6 8.0 %collective-permute-start.19 = (bf16[48,1536]{1,0:T(8,128)(2,1)}, bf16[48,1536]{1,0:T(8,128)(2,1)S(1)}, u32[]{:S(2)}, u32[]{:S(2)}) collective-permute-start(bf16[48,1536]{1,0:T(8,128)(2,1)} %reduce-scatter.5.cloned.1.call-done), channel_id=1, source_target_pairs={{0,4},{2,6},{4,0},{6,2},{1,5},{3,7},{5,1},{7,3},{8,12},{10,14},{12... | collective-permute-start | bytes 442376 | tf_op jit(solution)/shard_map/ppermute | solution.py:67
  433.3 5.4 collective-permute-start.20
  509.9 10.4 %collective-permute-start.30 = (bf16[48,3072]{1,0:T(8,128)(2,1)}, bf16[48,3072]{1,0:T(8,128)(2,1)S(1)}, u32[]{:S(2)}, u32[]{:S(2)}) collective-permute-start(bf16[48,3072]{1,0:T(8,128)(2,1)} %reduce-scatter.11.cloned.1.call-done), channel_id=1, source_target_pairs={{0,2},{2,4},{4,6},{6,0},{1,3},{3,5},{5,7},{7,1},{8,10},{10,12},{12... | collective-permute-start | bytes 884744 | tf_op jit(solution)/shard_map/ppermute | solution.py:67
  511.4 14.4 %collective-permute-start.31 = (bf16[48,3072]{1,0:T(8,128)(2,1)}, bf16[48,3072]{1,0:T(8,128)(2,1)S(1)}, u32[]{:S(2)}, u32[]{:S(2)}) collective-permute-start(bf16[48,3072]{1,0:T(8,128)(2,1)} %reduce-scatter.11.cloned.1.call-done), channel_id=1, source_target_pairs={{0,4},{2,6},{4,0},{6,2},{1,5},{3,7},{5,1},{7,3},{8,12},{10,14},{12... | collective-permute-start | bytes 884744 | tf_op jit(solution)/shard_map/ppermute | solution.py:67
  514.1 11.7 %collective-permute-start.32 = (bf16[48,3072]{1,0:T(8,128)(2,1)}, bf16[48,3072]{1,0:T(8,128)(2,1)S(1)}, u32[]{:S(2)}, u32[]{:S(2)}) collective-permute-start(bf16[48,3072]{1,0:T(8,128)(2,1)} %reduce-scatter.11.cloned.1.call-done), channel_id=1, source_target_pairs={{0,6},{2,0},{4,2},{6,4},{1,7},{3,1},{5,3},{7,5},{8,14},{10,8},{12,... | collective-permute-start | bytes 884744 | tf_op jit(solution)/shard_map/ppermute | solution.py:67
  590.9 10.4 %collective-permute-start.27 = (bf16[48,3072]{1,0:T(8,128)(2,1)}, bf16[48,3072]{1,0:T(8,128)(2,1)S(1)}, u32[]{:S(2)}, u32[]{:S(2)}) collective-permute-start(bf16[48,3072]{1,0:T(8,128)(2,1)} %reduce-scatter.9.cloned.1.call-done), channel_id=1, source_target_pairs={{0,2},{2,4},{4,6},{6,0},{1,3},{3,5},{5,7},{7,1},{8,10},{10,12},{12... | collective-permute-start | bytes 884744 | tf_op jit(solution)/shard_map/ppermute | solution.py:67
  592.3 14.4 %collective-permute-start.28 = (bf16[48,3072]{1,0:T(8,128)(2,1)}, bf16[48,3072]{1,0:T(8,128)(2,1)S(1)}, u32[]{:S(2)}, u32[]{:S(2)}) collective-permute-start(bf16[48,3072]{1,0:T(8,128)(2,1)} %reduce-scatter.9.cloned.1.call-done), channel_id=1, source_target_pairs={{0,4},{2,6},{4,0},{6,2},{1,5},{3,7},{5,1},{7,3},{8,12},{10,14},{12... | collective-permute-start | bytes 884744 | tf_op jit(solution)/shard_map/ppermute | solution.py:67
  595.0 11.7 %collective-permute-start.29 = (bf16[48,3072]{1,0:T(8,128)(2,1)}, bf16[48,3072]{1,0:T(8,128)(2,1)S(1)}, u32[]{:S(2)}, u32[]{:S(2)}) collective-permute-start(bf16[48,3072]{1,0:T(8,128)(2,1)} %reduce-scatter.9.cloned.1.call-done), channel_id=1, source_target_pairs={{0,6},{2,0},{4,2},{6,4},{1,7},{3,1},{5,3},{7,5},{8,14},{10,8},{12,... | collective-permute-start | bytes 884744 | tf_op jit(solution)/shard_map/ppermute | solution.py:67
  (112 other events, 574.6 us)
Sparse Core Ops, SparseCore 0:
  13.5 67.7 all-gather.2
  83.9 64.6 all-gather.4
  271.8 79.7 reduce-scatter.6
  354.8 74.2 reduce-scatter.4
  432.3 77.6 reduce-scatter.10
  513.1 77.6 reduce-scatter.8
where the time goes:
time: 627 us; the launch traced here: 617 us
  waiting for transfers between devices  323 us (52%)
  local copies, waits for them, and re-layouts  82.9 us (13%)
  starting transfers between devices  76.2 us (12%)
  matrix products  68.4 us (11%)
  other arithmetic  50.4 us (8%)
  between operations  16.2 us (3%)
    reduce_scatter x4, waiting for transfers between devices, scatter(): return lax.psum_scatter(packed, 'shard', scatter_dimension=0, tiled=True)  176 us
    all_gather x2, waiting for transfers between devices, per_device(): gathered.append(lax.all_gather(packed, 'shard', axis=0, tiled=True))  49.1 us
    dot_general x24, matrix products, dot(): lax.dot_general(left, right, (((left_dim,), (right_dim,)), ((), ())), pre...  46.1 us
    ppermute x15, starting transfers between devices, context_sum(): lax.ppermute(part, 'context', [(i, (i + steps) % size) for i in range(siz...  31.3 us
    ppermute x4, waiting for transfers between devices, from_after(): lax.ppermute(block, 'context', [(i + steps, i) for i in range(size - step...  29.2 us
    ppermute x15, waiting for transfers between devices, context_sum(): lax.ppermute(part, 'context', [(i, (i + steps) % size) for i in range(siz...  25.6 us
    ppermute x6, waiting for transfers between devices, from_before(): lax.ppermute(block, 'context', [(i, i + steps) for i in range(size - step...  25 us
    ppermute x6, starting transfers between devices, from_before(): lax.ppermute(block, 'context', [(i, i + steps) for i in range(size - step...  24.3 us
  transfers between devices with their start and end apart: 41, of which 26 were waited for; matrix products, arithmetic and copies ran while one was open for 19% of the time, Pallas kernels for 0%

commit v1 on v0

--- a/solution.py
+++ b/solution.py
@@ -10,6 +10,11 @@
 MASKED = -1e30
 HALF = jnp.bfloat16
 FULL = jnp.float32
+
+
+def gather_by_exchange(value, axis, dim):
+    copies = jnp.concatenate([value] * lax.axis_size(axis), axis=dim)
+    return lax.all_to_all(copies, axis, dim, dim, tiled=True)
 
 
 def gelu_value(preact):
@@ -114,7 +119,7 @@
             ],
             axis=1,
         )
-        gathered.append(lax.all_gather(packed, "shard", axis=0, tiled=True))
+        gathered.append(gather_by_exchange(packed, "shard", 0))
     small_parts = [norm_gains, offsets, head_bias, hidden_bias]
     small_sizes = [part.size for part in small_parts]
     small_total = sum(small_sizes)

time: 627 us -> 819 us (1.31)
  local copies, waits for them, and re-layouts: 82.9 us -> 173 us
  waiting for transfers between devices: 323 us -> 383 us
  matrix products: 68.4 us -> 85.4 us
  starting transfers between devices: 76.2 us -> 91.1 us
  other arithmetic: 50.4 us -> 58.9 us
    all_to_all x0 -> x2, waiting for transfers between devices: none -> 143 us  [gather_by_exchange(): return lax.all_to_all(copies, axis, dim, dim, tiled=True)]
    unnamed x253 -> x292, local copies, waits for them, and re-layouts: 22.8 us -> 108 us
    all_gather x2 -> x0, waiting for transfers between devices: 49.1 us -> none  [per_device(): gathered.append(lax.all_gather(packed, 'shard', axis=0, tiled=True))]
    reduce_scatter x4, waiting for transfers between devices: 176 us -> 162 us  [scatter(): return lax.psum_scatter(packed, 'shard', scatter_dimension=0, tiled=True)]
    all_to_all x0 -> x2, starting transfers between devices: none -> 12.8 us  [gather_by_exchange(): return lax.all_to_all(copies, axis, dim, dim, tiled=True)]
    dot_general x24, matrix products: 46.1 us -> 57.6 us  [dot(): lax.dot_general(left, right, (((left_dim,), (right_dim,)), ((), ())), pre...]
  transfers between devices with their start and end apart: 41 -> 41, of which waited for: 26 -> 26; matrix products, arithmetic and copies ran while one was open for 19% -> 28% of each run, Pallas kernels for 0% -> 0%
where the time goes in v1:
time: 819 us; the launch traced here: 807 us
  waiting for transfers between devices  383 us (47%)
  local copies, waits for them, and re-layouts  173 us (21%)
  starting transfers between devices  91.1 us (11%)
  matrix products  85.4 us (10%)
  other arithmetic  58.9 us (7%)
  between operations  15.4 us (2%)
    reduce_scatter x4, waiting for transfers between devices, scatter(): return lax.psum_scatter(packed, 'shard', scatter_dimension=0, tiled=True)  162 us
    all_to_all x2, waiting for transfers between devices, gather_by_exchange(): return lax.all_to_all(copies, axis, dim, dim, tiled=True)  143 us
    unnamed x292, local copies, waits for them, and re-layouts  108 us
    dot_general x24, matrix products, dot(): lax.dot_general(left, right, (((left_dim,), (right_dim,)), ((), ())), pre...  57.6 us
    ppermute x15, starting transfers between devices, context_sum(): lax.ppermute(part, 'context', [(i, (i + steps) % size) for i in range(siz...  31.9 us
    ppermute x6, starting transfers between devices, from_before(): lax.ppermute(block, 'context', [(i, i + steps) for i in range(size - step...  25.4 us
    ppermute x4, waiting for transfers between devices, from_after(): lax.ppermute(block, 'context', [(i + steps, i) for i in range(size - step...  25 us
    ppermute x15, waiting for transfers between devices, context_sum(): lax.ppermute(part, 'context', [(i, (i + steps) % size) for i in range(siz...  24.8 us
  transfers between devices with their start and end apart: 41, of which 26 were waited for; matrix products, arithmetic and copies ran while one was open for 28% of the time, Pallas kernels for 0%

profile of v1, /device:TPU:0, one launch (start us, length us, event | category | flops | bytes accessed | tf_op | source)
XLA Modules:
  0.0 806.6 jit_solution(5356846772452119528)
XLA Ops:
  11.4 8.0 all-to-all-start
  112.3 7.4 all-to-all-start.1
  119.7 5.1 collective-permute-start.2
  130.1 93.4 %all-to-all-done.1 = bf16[16,48,4608]{2,1,0:T(8,128)(2,1)} async-done(((bf16[16,48,4608]{2,1,0:T(8,128)(2,1)}), bf16[16,48,4608]{2,1,0:T(8,128)(2,1)}, u32[]{:S(2)}, u32[]{:S(2)}) %all-to-all-start.1) | async-done | bytes 7077920 | tf_op jit(solution)/shard_map/all_to_all | solution.py:17
  223.5 5.4 all-to-all-start.2
  231.7 5.1 collective-permute-start
  236.9 3.3 collective-permute-start.1
  240.6 5.8 collective-permute-done
  247.1 4.5 collective-permute-done.1
  271.2 4.2 fusion.15
  281.1 49.2 %all-to-all-done.2 = bf16[16,48,4608]{2,1,0:T(8,128)(2,1)} async-done(((bf16[16,48,4608]{2,1,0:T(8,128)(2,1)}), bf16[16,48,4608]{2,1,0:T(8,128)(2,1)}, u32[]{:S(2)}, u32[]{:S(2)}) %all-to-all-start.2) | async-done | bytes 7077920 | tf_op jit(solution)/shard_map/all_to_all | solution.py:17
  333.6 5.9 collective-permute-start.6
  339.4 3.4 collective-permute-start.7
  344.6 3.9 collective-permute-done.6
  348.5 4.4 collective-permute-done.7
  383.1 4.2 fusion.135
  388.3 3.3 fusion.45
  392.0 3.6 fusion.9
  398.5 4.0 fusion.119
  407.6 3.3 fusion.80
  410.9 3.7 multiply_convert_fusion.1
  417.2 2.8 fusion.100
  428.1 2.8 fusion.130
  433.5 6.3 collective-permute-done.11
  439.8 3.1 collective-permute-done.12
  451.9 3.9 fusion.136
  456.7 3.2 fusion.42
  473.3 2.7 copy.195
  481.4 2.7 copy.194
  493.4 12.8 %collective-permute-done.15 = bf16[2,128,768]{2,1,0:T(8,128)(2,1)} collective-permute-done((bf16[2,128,768]{2,1,0:T(8,128)(2,1)}, bf16[2,128,768]{2,1,0:T(8,128)(2,1)}, u32[]{:S(2)}, u32[]{:S(2)}) %collective-permute-start.15) | collective-permute-done | bytes 393248 | tf_op jit(solution)/shard_map/ppermute | solution.py:65
  506.2 2.9 collective-permute-done.16
  519.3 2.7 pad_maximum_fusion.1
  526.8 2.7 pad_maximum_fusion
  556.1 5.1 all-to-all-start.3
  561.3 7.6 all-to-all-done.3
  568.9 7.4 collective-permute-start.24
  576.4 2.8 collective-permute-start.26
  581.7 3.8 collective-permute-start.22
  591.9 27.3 %reduce-scatter.5.cloned.1.call-done = bf16[48,1536]{1,0:T(8,128)(2,1)} async-done(((bf16[768,1536]{1,0:T(8,128)(2,1)}), bf16[48,1536]{1,0:T(8,128)(2,1)}) %reduce-scatter.5.cloned.1.call-update) | async-done | bytes 147472 | tf_op jit(solution)/shard_map/reduce_scatter | solution.py:217
  620.7 2.7 collective-permute-start.19
  629.8 70.4 %reduce-scatter.11.cloned.1.call-done = bf16[48,3072]{1,0:T(8,128)(2,1)} async-done(((bf16[768,3072]{1,0:T(8,128)(2,1)}), bf16[48,3072]{1,0:T(8,128)(2,1)}) %reduce-scatter.11.cloned.1.call-update) | async-done | bytes 294928 | tf_op jit(solution)/shard_map/reduce_scatter | solution.py:217
  701.7 2.7 collective-permute-start.31
  707.4 3.3 collective-permute-done.30
  710.6 5.4 collective-permute-done.31
  717.2 64.0 %reduce-scatter.9.cloned.1.call-done = bf16[48,3072]{1,0:T(8,128)(2,1)} async-done(((bf16[768,3072]{1,0:T(8,128)(2,1)}), bf16[48,3072]{1,0:T(8,128)(2,1)}) %reduce-scatter.9.cloned.1.call-update) | async-done | bytes 294928 | tf_op jit(solution)/shard_map/reduce_scatter | solution.py:217
  782.7 2.7 collective-permute-start.28
  786.9 4.7 collective-permute-done.27
  791.6 5.4 collective-permute-done.28
  (550 shorter events, 296.3 us)
Async XLA Ops:
  11.4 100.9 %all-to-all-start = ((bf16[16,8,128]{2,1,0:T(8,128)(2,1)}), bf16[16,8,128]{2,1,0:T(8,128)(2,1)S(1)}, u32[]{:S(2)}, u32[]{:S(2)}) async-start(bf16[16,8,128]{2,1,0:T(8,128)(2,1)} %broadcast_in_dim.34), calls=%async_computation | async-start | bytes 65536 | tf_op jit(solution)/shard_map/all_to_all | solution.py:132
  112.3 111.2 %all-to-all-start.1 = ((bf16[16,48,4608]{2,1,0:T(8,128)(2,1)}), bf16[16,48,4608]{2,1,0:T(8,128)(2,1)}, u32[]{:S(2)}, u32[]{:S(2)}) async-start(bf16[16,48,4608]{2,1,0:T(8,128)(2,1)} %bitcast.14), calls=%async_computation.1 | async-start | bytes 14155776 | tf_op jit(solution)/shard_map/all_to_all | solution.py:17
  119.7 120.5 %collective-permute-start.2 = (s32[2,128]{1,0:T(2,128)S(1)}, s32[2,128]{1,0:T(2,128)S(1)}, u32[]{:S(2)}, u32[]{:S(2)}) collective-permute-start(s32[2,128]{1,0:T(2,128)S(1)} %copy-done.72), channel_id=1, source_target_pairs={{0,4},{2,6},{1,5},{3,7},{8,12},{10,14},{9,13},{11,15},{16,20},{18,... | collective-permute-start | bytes 3080 | tf_op jit(solution)/shard_map/ppermute | solution.py:60
  124.8 115.4 %collective-permute-start.3 = (s32[2,128]{1,0:T(2,128)S(1)}, s32[2,128]{1,0:T(2,128)S(1)}, u32[]{:S(2)}, u32[]{:S(2)}) collective-permute-start(s32[2,128]{1,0:T(2,128)S(1)} %copy-done.72), channel_id=1, source_target_pairs={{0,2},{2,4},{4,6},{1,3},{3,5},{5,7},{8,10},{10,12},{12,14},{9,11},... | collective-permute-start | bytes 3080 | tf_op jit(solution)/shard_map/ppermute | solution.py:60
  127.5 95.9 %copy-start.58 = (f32[256]{0:T(256)}, f32[256]{0:T(256)S(1)}, u32[]{:S(2)}) copy-start(f32[256]{0:T(256)S(1)} %get-tuple-element.259) | copy-start | bytes 3076
  127.8 95.7 %copy-start.60 = (f32[256]{0:T(256)}, f32[256]{0:T(256)S(1)}, u32[]{:S(2)}) copy-start(f32[256]{0:T(256)S(1)} %rsqrt_bitcast_fusion) | copy-start | bytes 3076
  129.2 94.3 %copy-start.40 = (f32[768]{0:T(1024)}, f32[768]{0:T(1024)S(1)}, u32[]{:S(2)}) copy-start(f32[768]{0:T(1024)S(1)} %mul.315) | copy-start | bytes 9220
  130.1 99.5 %copy-start.29 = (bf16[256,768]{1,0:T(8,128)(2,1)}, bf16[256,768]{1,0:T(8,128)(2,1)S(1)}, u32[]{:S(2)}) copy-start(bf16[256,768]{1,0:T(8,128)(2,1)S(1)} %add_convert_fusion.3) | copy-start | bytes 1179652
  223.5 106.8 %all-to-all-start.2 = ((bf16[16,48,4608]{2,1,0:T(8,128)(2,1)}), bf16[16,48,4608]{2,1,0:T(8,128)(2,1)}, u32[]{:S(2)}, u32[]{:S(2)}) async-start(bf16[16,48,4608]{2,1,0:T(8,128)(2,1)} %bitcast.413), calls=%async_computation.2 | async-start | bytes 14155776 | tf_op jit(solution)/shard_map/all_to_all | solution.py:17
  228.9 352.8 %reduce-scatter.7.cloned.1.call-start = ((), (), s32[]{:S(2)}) async-start(), calls=%async_computation.9 | async-start | bytes 2506752 | tf_op jit(solution)/shard_map/reduce_scatter | solution.py:217
  231.7 14.7 %collective-permute-start = (bf16[2,128,768]{2,1,0:T(8,128)(2,1)S(1)}, bf16[2,128,768]{2,1,0:T(8,128)(2,1)S(1)}, u32[]{:S(2)}, u32[]{:S(2)}) collective-permute-start(bf16[2,128,768]{2,1,0:T(8,128)(2,1)S(1)} %bitcast.432), channel_id=1, source_target_pairs={{0,4},{2,6},{1,5},{3,7},{8,12},{10,14},{9,13},{11,15},{16,20},{18,... | collective-permute-start | bytes 1179656 | tf_op jit(solution)/shard_map/ppermute | solution.py:60
  236.9 14.8 %collective-permute-start.1 = (bf16[2,128,768]{2,1,0:T(8,128)(2,1)S(1)}, bf16[2,128,768]{2,1,0:T(8,128)(2,1)}, u32[]{:S(2)}, u32[]{:S(2)}) collective-permute-start(bf16[2,128,768]{2,1,0:T(8,128)(2,1)S(1)} %bitcast.433), channel_id=1, source_target_pairs={{0,2},{2,4},{4,6},{1,3},{3,5},{5,7},{8,10},{10,12},{12,14},{9,11},... | collective-permute-start | bytes 1179656 | tf_op jit(solution)/shard_map/ppermute | solution.py:60
  262.6 3.5 collective-permute-start.4
  275.4 2.8 collective-permute-start.5
  276.0 63.4 %copy-start.44 = (f32[768]{0:T(1024)}, f32[768]{0:T(1024)S(1)}, u32[]{:S(2)}) copy-start(f32[768]{0:T(1024)S(1)} %mul.335) | copy-start | bytes 9220
  276.1 63.3 %copy-start.68 = (f32[768]{0:T(1024)}, f32[768]{0:T(1024)S(1)}, u32[]{:S(2)}) copy-start(f32[768]{0:T(1024)S(1)} %add.345) | copy-start | bytes 9220
  280.0 59.5 %copy-start.54 = (f32[256]{0:T(256)}, f32[256]{0:T(256)S(1)}, u32[]{:S(2)}) copy-start(f32[256]{0:T(256)S(1)} %broadcast_multiply_fusion.9) | copy-start | bytes 3076
  333.6 15.0 %collective-permute-start.6 = (bf16[2,128,768]{2,1,0:T(8,128)(2,1)}, bf16[2,128,768]{2,1,0:T(8,128)(2,1)}, u32[]{:S(2)}, u32[]{:S(2)}) collective-permute-start(bf16[2,128,768]{2,1,0:T(8,128)(2,1)} %bitcast.34), channel_id=1, source_target_pairs={{0,4},{2,6},{1,5},{3,7},{8,12},{10,14},{9,13},{11,15},{16,20},{18,... | collective-permute-start | bytes 1179656 | tf_op jit(solution)/shard_map/ppermute | solution.py:60
  339.4 13.5 %collective-permute-start.7 = (bf16[2,128,768]{2,1,0:T(8,128)(2,1)}, bf16[2,128,768]{2,1,0:T(8,128)(2,1)}, u32[]{:S(2)}, u32[]{:S(2)}) collective-permute-start(bf16[2,128,768]{2,1,0:T(8,128)(2,1)} %bitcast.34), channel_id=1, source_target_pairs={{0,2},{2,4},{4,6},{1,3},{3,5},{5,7},{8,10},{10,12},{12,14},{9,11},... | collective-permute-start | bytes 1179656 | tf_op jit(solution)/shard_map/ppermute | solution.py:60
  369.4 8.4 %collective-permute-start.8 = (f32[256,768]{1,0:T(8,128)}, f32[256,768]{1,0:T(8,128)}, u32[]{:S(2)}, u32[]{:S(2)}) collective-permute-start(f32[256,768]{1,0:T(8,128)} %fusion.71), channel_id=1, source_target_pairs={{0,1},{1,0},{2,3},{3,2},{4,5},{5,4},{6,7},{7,6},{8,9},{9,8},{10,11... | collective-permute-start | bytes 2359304 | tf_op jit(solution)/shard_map/ppermute | solution.py:54
  391.5 4.4 collective-permute-start.10
  395.7 2.8 collective-permute-start.9
  425.3 14.5 %collective-permute-start.11 = (bf16[2,128,768]{2,1,0:T(8,128)(2,1)}, bf16[2,128,768]{2,1,0:T(8,128)(2,1)}, u32[]{:S(2)}, u32[]{:S(2)}) collective-permute-start(bf16[2,128,768]{2,1,0:T(8,128)(2,1)} %get-tuple-element.106), channel_id=1, source_target_pairs={{2,0},{4,2},{6,4},{3,1},{5,3},{7,5},{10,8},{12,10},{14,12},{11,9},... | collective-permute-start | bytes 1179656 | tf_op jit(solution)/shard_map/ppermute | solution.py:65
  426.8 16.2 %collective-permute-start.12 = (bf16[2,128,768]{2,1,0:T(8,128)(2,1)}, bf16[2,128,768]{2,1,0:T(8,128)(2,1)}, u32[]{:S(2)}, u32[]{:S(2)}) collective-permute-start(bf16[2,128,768]{2,1,0:T(8,128)(2,1)} %get-tuple-element.107), channel_id=1, source_target_pairs={{4,0},{6,2},{5,1},{7,3},{12,8},{14,10},{13,9},{15,11},{20,16},{22,... | collective-permute-start | bytes 1179656 | tf_op jit(solution)/shard_map/ppermute | solution.py:65
  447.7 2.1 collective-permute-start.13
  460.0 2.6 collective-permute-start.14
  462.1 157.1 %reduce-scatter.5.cloned.1.call-start = ((), (), s32[]{:S(2)}) async-start(), calls=%async_computation.8 | async-start | bytes 2506752 | tf_op jit(solution)/shard_map/reduce_scatter | solution.py:217
  486.7 19.5 %collective-permute-start.15 = (bf16[2,128,768]{2,1,0:T(8,128)(2,1)}, bf16[2,128,768]{2,1,0:T(8,128)(2,1)}, u32[]{:S(2)}, u32[]{:S(2)}) collective-permute-start(bf16[2,128,768]{2,1,0:T(8,128)(2,1)} %get-tuple-element.104), channel_id=1, source_target_pairs={{2,0},{4,2},{6,4},{3,1},{5,3},{7,5},{10,8},{12,10},{14,12},{11,9},... | collective-permute-start | bytes 1179656 | tf_op jit(solution)/shard_map/ppermute | solution.py:65
  488.0 21.1 %collective-permute-start.16 = (bf16[2,128,768]{2,1,0:T(8,128)(2,1)S(1)}, bf16[2,128,768]{2,1,0:T(8,128)(2,1)}, u32[]{:S(2)}, u32[]{:S(2)}) collective-permute-start(bf16[2,128,768]{2,1,0:T(8,128)(2,1)S(1)} %get-tuple-element.105), channel_id=1, source_target_pairs={{4,0},{6,2},{5,1},{7,3},{12,8},{14,10},{13,9},{15,11},{20,16},{22,... | collective-permute-start | bytes 1179656 | tf_op jit(solution)/shard_map/ppermute | solution.py:65
  514.6 185.6 %reduce-scatter.11.cloned.1.call-start = ((), (), s32[]{:S(2)}) async-start(), calls=%async_computation.11 | async-start | bytes 5013504 | tf_op jit(solution)/shard_map/reduce_scatter | solution.py:217
  522.0 259.1 %reduce-scatter.9.cloned.1.call-start = ((), (), s32[]{:S(2)}) async-start(), calls=%async_computation.10 | async-start | bytes 5013504 | tf_op jit(solution)/shard_map/reduce_scatter | solution.py:217
  544.6 7.7 collective-permute-start.17
  556.1 12.8 %all-to-all-start.3 = ((f32[16,8,128]{2,1,0:T(8,128)}), f32[16,8,128]{2,1,0:T(8,128)S(1)}, u32[]{:S(2)}, u32[]{:S(2)}) async-start(f32[16,8,128]{2,1,0:T(8,128)} %bitcast.127), calls=%async_computation.5 | async-start | bytes 131072 | tf_op jit(solution)/shard_map/all_to_all | solution.py:318
  568.9 12.1 %collective-permute-start.24 = (f32[8,128]{1,0:T(8,128)S(1)}, f32[8,128]{1,0:T(8,128)S(1)}, u32[]{:S(2)}, u32[]{:S(2)}) collective-permute-start(f32[8,128]{1,0:T(8,128)S(1)} %reduce_sum.395), channel_id=1, source_target_pairs={{0,2},{2,4},{4,6},{6,0},{1,3},{3,5},{5,7},{7,1},{8,10},{10,12},{12... | collective-permute-start | bytes 12296 | tf_op jit(solution)/shard_map/ppermute | solution.py:72
  576.4 5.1 collective-permute-start.25
  576.4 5.1 collective-permute-start.26
  581.6 7.7 collective-permute-start.21
  581.7 8.7 %collective-permute-start.22 = (bf16[48,1536]{1,0:T(8,128)(2,1)}, bf16[48,1536]{1,0:T(8,128)(2,1)S(1)}, u32[]{:S(2)}, u32[]{:S(2)}) collective-permute-start(bf16[48,1536]{1,0:T(8,128)(2,1)} %reduce-scatter.7.cloned.1.call-done), channel_id=1, source_target_pairs={{0,4},{2,6},{4,0},{6,2},{1,5},{3,7},{5,1},{7,3},{8,12},{10,14},{12... | collective-permute-start | bytes 442376 | tf_op jit(solution)/shard_map/ppermute | solution.py:72
  585.6 5.4 collective-permute-start.23
  619.2 7.9 collective-permute-start.18
  620.7 7.9 collective-permute-start.19
  623.4 5.4 collective-permute-start.20
  700.2 10.4 %collective-permute-start.30 = (bf16[48,3072]{1,0:T(8,128)(2,1)}, bf16[48,3072]{1,0:T(8,128)(2,1)S(1)}, u32[]{:S(2)}, u32[]{:S(2)}) collective-permute-start(bf16[48,3072]{1,0:T(8,128)(2,1)} %reduce-scatter.11.cloned.1.call-done), channel_id=1, source_target_pairs={{0,2},{2,4},{4,6},{6,0},{1,3},{3,5},{5,7},{7,1},{8,10},{10,12},{12... | collective-permute-start | bytes 884744 | tf_op jit(solution)/shard_map/ppermute | solution.py:72
  701.7 14.4 %collective-permute-start.31 = (bf16[48,3072]{1,0:T(8,128)(2,1)}, bf16[48,3072]{1,0:T(8,128)(2,1)S(1)}, u32[]{:S(2)}, u32[]{:S(2)}) collective-permute-start(bf16[48,3072]{1,0:T(8,128)(2,1)} %reduce-scatter.11.cloned.1.call-done), channel_id=1, source_target_pairs={{0,4},{2,6},{4,0},{6,2},{1,5},{3,7},{5,1},{7,3},{8,12},{10,14},{12... | collective-permute-start | bytes 884744 | tf_op jit(solution)/shard_map/ppermute | solution.py:72
  704.4 11.6 %collective-permute-start.32 = (bf16[48,3072]{1,0:T(8,128)(2,1)}, bf16[48,3072]{1,0:T(8,128)(2,1)S(1)}, u32[]{:S(2)}, u32[]{:S(2)}) collective-permute-start(bf16[48,3072]{1,0:T(8,128)(2,1)} %reduce-scatter.11.cloned.1.call-done), channel_id=1, source_target_pairs={{0,6},{2,0},{4,2},{6,4},{1,7},{3,1},{5,3},{7,5},{8,14},{10,8},{12,... | collective-permute-start | bytes 884744 | tf_op jit(solution)/shard_map/ppermute | solution.py:72
  781.2 10.4 %collective-permute-start.27 = (bf16[48,3072]{1,0:T(8,128)(2,1)}, bf16[48,3072]{1,0:T(8,128)(2,1)S(1)}, u32[]{:S(2)}, u32[]{:S(2)}) collective-permute-start(bf16[48,3072]{1,0:T(8,128)(2,1)} %reduce-scatter.9.cloned.1.call-done), channel_id=1, source_target_pairs={{0,2},{2,4},{4,6},{6,0},{1,3},{3,5},{5,7},{7,1},{8,10},{10,12},{12... | collective-permute-start | bytes 884744 | tf_op jit(solution)/shard_map/ppermute | solution.py:72
  782.7 14.4 %collective-permute-start.28 = (bf16[48,3072]{1,0:T(8,128)(2,1)}, bf16[48,3072]{1,0:T(8,128)(2,1)S(1)}, u32[]{:S(2)}, u32[]{:S(2)}) collective-permute-start(bf16[48,3072]{1,0:T(8,128)(2,1)} %reduce-scatter.9.cloned.1.call-done), channel_id=1, source_target_pairs={{0,4},{2,6},{4,0},{6,2},{1,5},{3,7},{5,1},{7,3},{8,12},{10,14},{12... | collective-permute-start | bytes 884744 | tf_op jit(solution)/shard_map/ppermute | solution.py:72
  785.4 11.6 %collective-permute-start.29 = (bf16[48,3072]{1,0:T(8,128)(2,1)}, bf16[48,3072]{1,0:T(8,128)(2,1)S(1)}, u32[]{:S(2)}, u32[]{:S(2)}) collective-permute-start(bf16[48,3072]{1,0:T(8,128)(2,1)} %reduce-scatter.9.cloned.1.call-done), channel_id=1, source_target_pairs={{0,6},{2,0},{4,2},{6,4},{1,7},{3,1},{5,3},{7,5},{8,14},{10,8},{12,... | collective-permute-start | bytes 884744 | tf_op jit(solution)/shard_map/ppermute | solution.py:72
  (69 other events, 968.7 us)
Sparse Core Ops, SparseCore 0:
  462.2 79.3 reduce-scatter.6
  544.9 74.2 reduce-scatter.4
  622.5 77.6 reduce-scatter.10
  703.4 77.7 reduce-scatter.8
